TPU v7x, 256 devices: a whole 4x4x8 slice. The times are simulated.
256 devices in a mesh: cuts: 16 (over z, core), rank: 16 (over x, y).
Axes of the slice: x: 4, y: 4, z: 8, core: 2. Of those that a mesh axis runs over, the one named last changes fastest.
Arguments:
- core_one: float32 [512, 320, 512], P('rank', 'cuts'), may hold values from -6 to 6
- core_two: float32 [512, 320, 512], P('rank', 'cuts'), may hold values from -0.25 to 0.25
- right_sketch: float32 [512, 128], replicated, may hold values from -0.25 to 0.25
- sketch_core: float32 [128, 320, 128], P(None, 'cuts'), may hold values from -0.03125 to 0.03125
Outputs:
- left_core: float32 [512, 320, 128], P('rank', 'cuts')
- middle_core: float32 [128, 320, 128], P('rank', 'cuts')
- carry: float32 [128, 512], replicated
All inputs are finite; a program needn't handle non-finite values.
Results may differ from a plain program's by a relative error of at most 0.00015.
Values sent between devices are 32-bit elements; how exact they have to be, the bound alone decides.
A program may use at most 64 MiB of HBM per device.

v0:
```python
import jax
import jax.numpy as jnp
from jax import lax
from jax.sharding import PartitionSpec as P

R = 512
NM = 320
L = 128


def orthonormalize(all_rows, own_rows, carry_of):
    highest = lax.Precision.HIGHEST
    local_gram = jnp.dot(
        own_rows.T, own_rows, precision=highest, preferred_element_type=jnp.float32
    )
    gram = lax.psum(local_gram, ("cuts", "rank"))
    factor = jnp.linalg.cholesky(gram)
    ortho = lax.linalg.triangular_solve(
        factor, all_rows, left_side=False, lower=True, transpose_a=True
    )
    carried = lax.psum(carry_of(ortho), ("cuts", "rank"))
    return (ortho, carried)


def on_device(core_one, core_two, right_sketch, sketch_core):
    highest = lax.Precision.HIGHEST
    local_rows, slices, width = core_one.shape
    sketch_width = right_sketch.shape[1]
    band = sketch_width // lax.axis_size("rank")
    sketched = jnp.einsum("anj,jc->anc", core_two, right_sketch, precision=highest)
    part_bridge = jnp.einsum("anc,bnc->ab", sketched, sketch_core, precision=highest)
    bridge_rows = lax.psum(part_bridge, "cuts")
    flat_one = core_one.reshape(local_rows * slices, width)
    first_rows = jnp.dot(
        flat_one,
        lax.all_gather(bridge_rows, "rank", axis=0, tiled=True),
        precision=highest,
        preferred_element_type=jnp.float32,
    )

    def first_carry_of(matrix):
        return jnp.dot(matrix.T, flat_one, precision=highest, preferred_element_type=jnp.float32)

    first_q, first_carry = orthonormalize(first_rows, first_rows, first_carry_of)
    left_core = (jnp.sqrt(jnp.float32(R * NM)) * first_q).reshape(local_rows, slices, sketch_width)
    offset = lax.axis_index("rank") * local_rows
    local_carry = lax.dynamic_slice_in_dim(first_carry, offset, local_rows, 1)
    projected = lax.psum_scatter(
        jnp.einsum("ba,ank->bnk", local_carry, core_two, precision=highest),
        "rank",
        scatter_dimension=0,
        tiled=True,
    )
    flat_two = projected.reshape(band * slices, width)
    second_rows = jnp.dot(
        flat_two, right_sketch, precision=highest, preferred_element_type=jnp.float32
    )

    def second_carry_of(matrix):
        return jnp.dot(matrix.T, flat_two, precision=highest, preferred_element_type=jnp.float32)

    second_flat, carry = orthonormalize(second_rows, second_rows, second_carry_of)
    second_q = second_flat.reshape(band, slices, sketch_width)
    middle_core = jnp.sqrt(jnp.float32(L * NM)) * second_q
    return (left_core, middle_core, carry)


def solution(mesh):
    placed = (P("rank", "cuts", None), P("rank", "cuts", None), P(), P(None, "cuts", None))
    return jax.shard_map(
        on_device,
        mesh=mesh,
        in_specs=placed,
        out_specs=(P("rank", "cuts", None), P("rank", "cuts", None), P()),
        check_vma=False,
    )
```

profile of v0, /device:TPU:2, one launch (start us, length us, event | category | flops | bytes accessed | tf_op | source)
XLA Modules:
  0.0 1233.6 jit_solution(7768651899658973247)
XLA Ops:
  7.2 1.3 copy-done
  8.5 2.1 fusion
  10.6 1.4 convolution_bitcast_fusion
  12.0 50.9 %psum.35 = f32[32,128]{1,0:T(8,128)S(1)} all-reduce(f32[32,128]{1,0:T(8,128)S(1)} %convolution_bitcast_fusion), channel_id=1, replica_groups=mesh['cuts'=16,'rank'=16] {'cuts'}, use_global_device_ids=true, to_apply=%region_0.0 | all-reduce | flops 4096 | bytes 32768 | tf_op jit(solution)/shard_map/psum | solution.py:32
  62.9 23.8 %all_gather.3 = f32[512,128]{1,0:T(8,128)S(1)} all-gather(f32[32,128]{1,0:T(8,128)S(1)} %psum.35), channel_id=1, replica_groups=mesh['cuts'=16,'rank'=16] {'rank'}, dimensions={0}, use_global_device_ids=true | all-gather | bytes 278528 | tf_op jit(solution)/shard_map/all_gather | solution.py:36
  86.7 3.2 copy.13
  89.9 1.5 reshape.29
  91.4 1.6 fusion.14
  92.9 1.1 fusion.15
  94.3 236.5 %all-reduce.5.cloned.1.call-done = f32[128,128]{0,1:T(8,128)} async-done(((f32[128,128]{0,1:T(8,128)}), f32[128,128]{0,1:T(8,128)}) %all-reduce.5.cloned.1.call-update) | async-done | bytes 65552 | tf_op jit(solution)/shard_map/psum | solution.py:16
  330.8 0.9 copy.15
  331.8 0.9 fusion.9
  332.6 11.7 cholesky.44
  345.0 0.7 fusion.2
  345.7 9.8 custom-call.8
  355.5 0.7 broadcast_multiply_fusion
  356.2 3.0 fusion.16
  359.2 251.8 %all-reduce.7.cloned.1.call-done = f32[128,512]{0,1:T(8,128)} async-done(((f32[128,512]{0,1:T(8,128)}), f32[128,512]{0,1:T(8,128)}) %all-reduce.7.cloned.1.call-update) | async-done | bytes 262160 | tf_op jit(solution)/shard_map/psum | solution.py:21
  611.0 6.8 fusion.10
  618.1 83.2 %reduce-scatter.2.cloned.1.call-done = f32[8,20,512]{2,0,1:T(8,128)} async-done(((f32[128,20,512]{2,0,1:T(8,128)}), f32[8,20,512]{2,0,1:T(8,128)}) %reduce-scatter.2.cloned.1.call-update) | async-done | bytes 327696 | tf_op jit(solution)/shard_map/reduce_scatter | solution.py:48
  701.3 1.2 copy.16
  703.0 1.1 fusion.18
  704.1 243.4 %all-reduce.9.cloned.1.call-done = f32[128,128]{0,1:T(8,128)} async-done(((f32[128,128]{0,1:T(8,128)}), f32[128,128]{0,1:T(8,128)}) %all-reduce.9.cloned.1.call-update) | async-done | bytes 65552 | tf_op jit(solution)/shard_map/psum | solution.py:16
  947.6 0.9 copy.18
  948.5 0.9 fusion.6
  949.3 11.7 cholesky.55
  961.7 0.7 fusion.3
  962.4 9.8 custom-call.9
  972.4 1.1 fusion.19
  973.6 0.8 copy.19
  975.1 250.3 %all-reduce.11.cloned.1.call-done = f32[128,512]{1,0:T(8,128)} async-done(((f32[128,512]{1,0:T(8,128)}), f32[128,512]{1,0:T(8,128)}) %all-reduce.11.cloned.1.call-update) | async-done | bytes 262160 | tf_op jit(solution)/shard_map/psum | solution.py:21
  1225.4 1.7 copy.29
  (25 shorter events, 3.4 us)
Async XLA Ops:
  7.2 1.3 copy-start
  7.2 3.4 copy-start.1
  7.2 323.6 %all-reduce.5.cloned.1.call-start = ((), (), s32[]{:S(2)}) async-start(), calls=%async_computation.1 | async-start | bytes 131072 | tf_op jit(solution)/shard_map/psum | solution.py:16
  94.1 516.9 %all-reduce.7.cloned.1.call-start = ((), (), s32[]{:S(2)}) async-start(), calls=%async_computation.2 | async-start | bytes 524288 | tf_op jit(solution)/shard_map/psum | solution.py:21
  359.2 342.1 %reduce-scatter.2.cloned.1.call-start = ((), (), s32[]{:S(2)}) async-start(), calls=%async_computation.3 | async-start | bytes 5570560 | tf_op jit(solution)/shard_map/reduce_scatter | solution.py:48
  617.8 84.7 %copy-start.2 = (f32[512,128]{1,0:T(8,128)S(1)}, f32[512,128]{1,0:T(8,128)}, u32[]{:S(2)}) copy-start(f32[512,128]{1,0:T(8,128)} %param.7) | copy-start | bytes 786436
  617.8 329.7 %all-reduce.9.cloned.1.call-start = ((), (), s32[]{:S(2)}) async-start(), calls=%async_computation.4 | async-start | bytes 131072 | tf_op jit(solution)/shard_map/psum | solution.py:16
  704.1 521.3 %all-reduce.11.cloned.1.call-start = ((), (), s32[]{:S(2)}) async-start(), calls=%async_computation.5 | async-start | bytes 524288 | tf_op jit(solution)/shard_map/psum | solution.py:21
Sparse Core Ops, SparseCore 0:
  94.2 236.5 all-reduce.4
  359.3 251.6 all-reduce.6
  617.9 83.3 reduce-scatter.1
  707.3 240.2 all-reduce.8
  973.7 251.5 all-reduce.10
where the time goes:
time: 1230 us
  waiting for transfers between devices  1070 us (87%)
  blocking collectives  74.6 us (6%)
  other arithmetic  47.4 us (4%)
  matrix products  19.5 us (2%)
  between operations  13.9 us (1%)
    psum x2, waiting for transfers between devices, orthonormalize(): carried = lax.psum(carry_of(ortho), ('cuts', 'rank'))  502 us
    psum x2, waiting for transfers between devices, orthonormalize(): gram = lax.psum(local_gram, ('cuts', 'rank'))  480 us
    reduce_scatter x1, waiting for transfers between devices, on_device(): lax.psum_scatter(jnp.einsum('ba,ank->bnk', local_carry, core_two, precisi...  83.2 us
    psum x1, blocking collectives, on_device(): bridge_rows = lax.psum(part_bridge, 'cuts')  50.9 us
    another operation x6, other arithmetic, orthonormalize(): factor = jnp.linalg.cholesky(gram)  24.8 us
  transfers between devices with their start and end apart: 5, of which 5 were waited for; matrix products, arithmetic and copies ran while one was open for 0% of the time, Pallas kernels for 0%

commit v1 on v0

--- a/solution.py
+++ b/solution.py
@@ -6,6 +6,11 @@
 R = 512
 NM = 320
 L = 128
+
+
+def by_each_axis(value, one, other):
+    inner = lax.psum(value, one)
+    return lax.psum(inner, other)
 
 
 def orthonormalize(all_rows, own_rows, carry_of):
@@ -18,7 +23,7 @@
     ortho = lax.linalg.triangular_solve(
         factor, all_rows, left_side=False, lower=True, transpose_a=True
     )
-    carried = lax.psum(carry_of(ortho), ("cuts", "rank"))
+    carried = by_each_axis(carry_of(ortho), "rank", "cuts")
     return (ortho, carried)
 
 

time: 1230 us -> 1140 us (0.927)
  waiting for transfers between devices: 1070 us -> 972 us
    psum x2 -> x4, waiting for transfers between devices: 502 us -> 407 us  [the longest x2 223 us: by_each_axis(): return lax.psum(inner, other)]
  transfers between devices with their start and end apart: 5 -> 7, of which waited for: 5 -> 7; matrix products, arithmetic and copies ran while one was open for 0% -> 0% of each run, Pallas kernels for 0% -> 0%
where the time goes in v1:
time: 1140 us
  waiting for transfers between devices  972 us (85%)
  blocking collectives  74.6 us (7%)
  other arithmetic  47.4 us (4%)
  matrix products  19.5 us (2%)
  between operations  14.3 us (1%)
  local copies, waits for them, and re-layouts  12.2 us (1%)
    psum x2, waiting for transfers between devices, orthonormalize(): gram = lax.psum(local_gram, ('cuts', 'rank'))  480 us
    psum x2, waiting for transfers between devices, by_each_axis(): return lax.psum(inner, other)  223 us
    psum x2, waiting for transfers between devices, by_each_axis(): inner = lax.psum(value, one)  184 us
    reduce_scatter x1, waiting for transfers between devices, on_device(): lax.psum_scatter(jnp.einsum('ba,ank->bnk', local_carry, core_two, precisi...  84.9 us
    psum x1, blocking collectives, on_device(): bridge_rows = lax.psum(part_bridge, 'cuts')  50.9 us
    another operation x6, other arithmetic, orthonormalize(): factor = jnp.linalg.cholesky(gram)  24.8 us
    all_gather x1, blocking collectives, on_device(): lax.all_gather(bridge_rows, 'rank', axis=0, tiled=True)  23.8 us
  transfers between devices with their start and end apart: 7, of which 7 were waited for; matrix products, arithmetic and copies ran while one was open for 0% of the time, Pallas kernels for 0%

profile of v1, /device:TPU:2, one launch (start us, length us, event | category | flops | bytes accessed | tf_op | source)
XLA Modules:
  0.0 1140.6 jit_solution(18053771619772361479)
XLA Ops:
  7.2 1.3 copy-done
  8.5 2.1 fusion
  10.6 1.4 convolution_bitcast_fusion
  12.0 50.9 %psum.49 = f32[32,128]{1,0:T(8,128)S(1)} all-reduce(f32[32,128]{1,0:T(8,128)S(1)} %convolution_bitcast_fusion), channel_id=1, replica_groups=mesh['cuts'=16,'rank'=16] {'cuts'}, use_global_device_ids=true, to_apply=%region_0.0 | all-reduce | flops 4096 | bytes 32768 | tf_op jit(solution)/shard_map/psum | solution.py:37
  62.9 23.8 %all_gather.3 = f32[512,128]{1,0:T(8,128)S(1)} all-gather(f32[32,128]{1,0:T(8,128)S(1)} %psum.49), channel_id=1, replica_groups=mesh['cuts'=16,'rank'=16] {'rank'}, dimensions={0}, use_global_device_ids=true | all-gather | bytes 278528 | tf_op jit(solution)/shard_map/all_gather | solution.py:41
  86.7 3.2 copy.13
  89.9 1.5 reshape.29
  91.4 1.6 fusion.14
  92.9 1.1 fusion.15
  94.3 236.5 %all-reduce.7.cloned.1.call-done = f32[128,128]{0,1:T(8,128)} async-done(((f32[128,128]{0,1:T(8,128)}), f32[128,128]{0,1:T(8,128)}) %all-reduce.7.cloned.1.call-update) | async-done | bytes 65552 | tf_op jit(solution)/shard_map/psum | solution.py:21
  330.8 0.9 copy.15
  331.8 0.9 fusion.9
  332.6 11.7 %cholesky.44 = f32[128,128]{1,0:T(8,128)S(1)} custom-call(f32[128,128]{1,0:T(8,128)S(1)} %fusion.9), custom_call_target="Cholesky" | custom-call | tf_op jit(solution)/shard_map/jit(cholesky)/cholesky | solution.py:22
  345.7 9.8 custom-call.8
  355.5 0.7 broadcast_multiply_fusion
  356.2 3.0 fusion.16
  359.2 92.1 %all-reduce.9.cloned.1.call-done = f32[128,512]{0,1:T(8,128)} async-done(((f32[128,512]{0,1:T(8,128)}), f32[128,512]{0,1:T(8,128)}) %all-reduce.9.cloned.1.call-update) | async-done | bytes 262160 | tf_op jit(solution)/shard_map/psum | solution.py:12
  451.4 112.0 %all-reduce.11.cloned.1.call-done = f32[128,512]{0,1:T(8,128)} async-done(((f32[128,512]{0,1:T(8,128)}), f32[128,512]{0,1:T(8,128)}) %all-reduce.11.cloned.1.call-update) | async-done | bytes 262160 | tf_op jit(solution)/shard_map/psum | solution.py:13
  563.5 6.8 fusion.10
  570.6 84.9 %reduce-scatter.2.cloned.1.call-done = f32[8,20,512]{2,0,1:T(8,128)} async-done(((f32[128,20,512]{2,0,1:T(8,128)}), f32[8,20,512]{2,0,1:T(8,128)}) %reduce-scatter.2.cloned.1.call-update) | async-done | bytes 327696 | tf_op jit(solution)/shard_map/reduce_scatter | solution.py:53
  655.4 1.2 copy.16
  657.1 1.1 fusion.18
  658.2 243.5 %all-reduce.13.cloned.1.call-done = f32[128,128]{0,1:T(8,128)} async-done(((f32[128,128]{0,1:T(8,128)}), f32[128,128]{0,1:T(8,128)}) %all-reduce.13.cloned.1.call-update) | async-done | bytes 65552 | tf_op jit(solution)/shard_map/psum | solution.py:21
  901.8 0.9 copy.18
  902.7 0.9 fusion.6
  903.6 11.7 %cholesky.55 = f32[128,128]{1,0:T(8,128)S(1)} custom-call(f32[128,128]{1,0:T(8,128)S(1)} %fusion.6), custom_call_target="Cholesky" | custom-call | tf_op jit(solution)/shard_map/jit(cholesky)/cholesky | solution.py:22
  916.6 9.8 custom-call.9
  926.7 1.1 fusion.19
  927.9 92.1 %all-reduce.15.cloned.1.call-done = f32[128,512]{1,0:T(8,128)} async-done(((f32[128,512]{1,0:T(8,128)}), f32[128,512]{1,0:T(8,128)}) %all-reduce.15.cloned.1.call-update) | async-done | bytes 262160 | tf_op jit(solution)/shard_map/psum | solution.py:12
  1020.1 0.8 copy.19
  1021.5 110.6 %all-reduce.17.cloned.1.call-done = f32[128,512]{1,0:T(8,128)} async-done(((f32[128,512]{1,0:T(8,128)}), f32[128,512]{1,0:T(8,128)}) %all-reduce.17.cloned.1.call-update) | async-done | bytes 262160 | tf_op jit(solution)/shard_map/psum | solution.py:13
  1132.1 1.7 copy.31
  (31 shorter events, 4.9 us)
Async XLA Ops:
  7.2 1.3 copy-start
  7.2 3.4 copy-start.1
  7.2 323.6 %all-reduce.7.cloned.1.call-start = ((), (), s32[]{:S(2)}) async-start(), calls=%async_computation.1 | async-start | bytes 131072 | tf_op jit(solution)/shard_map/psum | solution.py:21
  94.1 357.3 %all-reduce.9.cloned.1.call-start = ((), (), s32[]{:S(2)}) async-start(), calls=%async_computation.2 | async-start | bytes 524288 | tf_op jit(solution)/shard_map/psum | solution.py:12
  359.2 204.3 %all-reduce.11.cloned.1.call-start = ((), (), s32[]{:S(2)}) async-start(), calls=%async_computation.3 | async-start | bytes 524288 | tf_op jit(solution)/shard_map/psum | solution.py:13
  451.4 204.1 %reduce-scatter.2.cloned.1.call-start = ((), (), s32[]{:S(2)}) async-start(), calls=%async_computation.4 | async-start | bytes 5570560 | tf_op jit(solution)/shard_map/reduce_scatter | solution.py:53
  570.3 86.4 %copy-start.2 = (f32[512,128]{1,0:T(8,128)S(1)}, f32[512,128]{1,0:T(8,128)}, u32[]{:S(2)}) copy-start(f32[512,128]{1,0:T(8,128)} %param.7) | copy-start | bytes 786436
  570.3 331.5 %all-reduce.13.cloned.1.call-start = ((), (), s32[]{:S(2)}) async-start(), calls=%async_computation.5 | async-start | bytes 131072 | tf_op jit(solution)/shard_map/psum | solution.py:21
  658.2 361.8 %all-reduce.15.cloned.1.call-start = ((), (), s32[]{:S(2)}) async-start(), calls=%async_computation.6 | async-start | bytes 524288 | tf_op jit(solution)/shard_map/psum | solution.py:12
  927.8 204.3 %all-reduce.17.cloned.1.call-start = ((), (), s32[]{:S(2)}) async-start(), calls=%async_computation.7 | async-start | bytes 524288 | tf_op jit(solution)/shard_map/psum | solution.py:13
Sparse Core Ops, SparseCore 0:
  94.2 236.5 all-reduce.6
  359.3 92.0 all-reduce.8
  453.7 109.7 all-reduce.10
  570.4 85.0 reduce-scatter.1
  661.4 240.3 all-reduce.12
  927.9 92.0 all-reduce.14
  1022.3 109.7 all-reduce.16

commit v2 on v0

--- a/solution.py
+++ b/solution.py
@@ -1,3 +1,4 @@
+import functools
 import jax
 import jax.numpy as jnp
 from jax import lax
@@ -8,12 +9,19 @@
 L = 128
 
 
+def start_the_hubs(v0, a_name, mesh_name):
+    return jax.lax.psum(jax.lax.psum(v0, axis_name=a_name), axis_name=mesh_name)
+
+
+work_set_on_mesh = functools.partial(start_the_hubs, a_name="cuts", mesh_name="rank")
+
+
 def orthonormalize(all_rows, own_rows, carry_of):
     highest = lax.Precision.HIGHEST
     local_gram = jnp.dot(
         own_rows.T, own_rows, precision=highest, preferred_element_type=jnp.float32
     )
-    gram = lax.psum(local_gram, ("cuts", "rank"))
+    gram = work_set_on_mesh(local_gram)
     factor = jnp.linalg.cholesky(gram)
     ortho = lax.linalg.triangular_solve(
         factor, all_rows, left_side=False, lower=True, transpose_a=True

time: 1230 us -> 1140 us (0.927)
  waiting for transfers between devices: 1070 us -> 974 us
    psum x2 -> x4, waiting for transfers between devices: 480 us -> 384 us  [start_the_hubs(): return jax.lax.psum(jax.lax.psum(v0, axis_name=a_name), axis_name=mesh_name)]
  transfers between devices with their start and end apart: 5 -> 7, of which waited for: 5 -> 7; matrix products, arithmetic and copies ran while one was open for 0% -> 0% of each run, Pallas kernels for 0% -> 0%
where the time goes in v2:
time: 1140 us
  waiting for transfers between devices  974 us (85%)
  blocking collectives  74.6 us (7%)
  other arithmetic  47.4 us (4%)
  matrix products  19.5 us (2%)
  between operations  14.3 us (1%)
  local copies, waits for them, and re-layouts  12.2 us (1%)
    psum x2, waiting for transfers between devices, orthonormalize(): carried = lax.psum(carry_of(ortho), ('cuts', 'rank'))  507 us
    psum x4, waiting for transfers between devices, start_the_hubs(): return jax.lax.psum(jax.lax.psum(v0, axis_name=a_name), axis_name=mesh_name)  384 us
    reduce_scatter x1, waiting for transfers between devices, on_device(): lax.psum_scatter(jnp.einsum('ba,ank->bnk', local_carry, core_two, precisi...  83.2 us
    psum x1, blocking collectives, on_device(): bridge_rows = lax.psum(part_bridge, 'cuts')  50.9 us
    another operation x6, other arithmetic, orthonormalize(): factor = jnp.linalg.cholesky(gram)  24.8 us
    all_gather x1, blocking collectives, on_device(): lax.all_gather(bridge_rows, 'rank', axis=0, tiled=True)  23.8 us
  transfers between devices with their start and end apart: 7, of which 7 were waited for; matrix products, arithmetic and copies ran while one was open for 0% of the time, Pallas kernels for 0%

profile of v2, /device:TPU:2, one launch (start us, length us, event | category | flops | bytes accessed | tf_op | source)
XLA Modules:
  0.0 1142.7 jit_solution(18340750666477256698)
XLA Ops:
  7.2 1.3 copy-done
  8.5 2.1 fusion
  10.6 1.4 convolution_bitcast_fusion
  12.0 50.9 %psum.49 = f32[32,128]{1,0:T(8,128)S(1)} all-reduce(f32[32,128]{1,0:T(8,128)S(1)} %convolution_bitcast_fusion), channel_id=1, replica_groups=mesh['cuts'=16,'rank'=16] {'cuts'}, use_global_device_ids=true, to_apply=%region_0.0 | all-reduce | flops 4096 | bytes 32768 | tf_op jit(solution)/shard_map/psum | solution.py:40
  62.9 23.8 %all_gather.3 = f32[512,128]{1,0:T(8,128)S(1)} all-gather(f32[32,128]{1,0:T(8,128)S(1)} %psum.49), channel_id=1, replica_groups=mesh['cuts'=16,'rank'=16] {'rank'}, dimensions={0}, use_global_device_ids=true | all-gather | bytes 278528 | tf_op jit(solution)/shard_map/all_gather | solution.py:44
  86.7 3.2 copy.13
  89.9 1.5 reshape.29
  91.4 1.6 fusion.14
  92.9 1.1 fusion.15
  94.1 96.5 %all-reduce.7.cloned.1.call-done = f32[128,128]{0,1:T(8,128)} async-done(((f32[128,128]{0,1:T(8,128)}), f32[128,128]{0,1:T(8,128)}) %all-reduce.7.cloned.1.call-update) | async-done | bytes 65552 | tf_op jit(solution)/shard_map/psum | solution.py:13
  190.9 93.5 %all-reduce.9.cloned.1.call-done = f32[128,128]{0,1:T(8,128)} async-done(((f32[128,128]{0,1:T(8,128)}), f32[128,128]{0,1:T(8,128)}) %all-reduce.9.cloned.1.call-update) | async-done | bytes 65552 | tf_op jit(solution)/shard_map/psum | solution.py:13
  284.4 0.9 copy.15
  285.4 0.9 fusion.9
  286.2 11.7 %cholesky.44 = f32[128,128]{1,0:T(8,128)S(1)} custom-call(f32[128,128]{1,0:T(8,128)S(1)} %fusion.9), custom_call_target="Cholesky" | custom-call | tf_op jit(solution)/shard_map/jit(cholesky)/cholesky | solution.py:25
  299.3 9.8 custom-call.8
  309.1 0.7 broadcast_multiply_fusion
  309.8 3.0 fusion.16
  312.8 254.1 %all-reduce.11.cloned.1.call-done = f32[128,512]{0,1:T(8,128)} async-done(((f32[128,512]{0,1:T(8,128)}), f32[128,512]{0,1:T(8,128)}) %all-reduce.11.cloned.1.call-update) | async-done | bytes 262160 | tf_op jit(solution)/shard_map/psum | solution.py:29
  567.0 6.8 fusion.10
  574.1 83.2 %reduce-scatter.2.cloned.1.call-done = f32[8,20,512]{2,0,1:T(8,128)} async-done(((f32[128,20,512]{2,0,1:T(8,128)}), f32[8,20,512]{2,0,1:T(8,128)}) %reduce-scatter.2.cloned.1.call-update) | async-done | bytes 327696 | tf_op jit(solution)/shard_map/reduce_scatter | solution.py:56
  657.3 1.2 copy.16
  658.9 1.1 fusion.18
  660.0 100.2 %all-reduce.13.cloned.1.call-done = f32[128,128]{0,1:T(8,128)} async-done(((f32[128,128]{0,1:T(8,128)}), f32[128,128]{0,1:T(8,128)}) %all-reduce.13.cloned.1.call-update) | async-done | bytes 65552 | tf_op jit(solution)/shard_map/psum | solution.py:13
  760.3 93.6 %all-reduce.15.cloned.1.call-done = f32[128,128]{0,1:T(8,128)} async-done(((f32[128,128]{0,1:T(8,128)}), f32[128,128]{0,1:T(8,128)}) %all-reduce.15.cloned.1.call-update) | async-done | bytes 65552 | tf_op jit(solution)/shard_map/psum | solution.py:13
  853.9 0.9 copy.18
  854.8 0.9 fusion.6
  855.7 11.7 %cholesky.55 = f32[128,128]{1,0:T(8,128)S(1)} custom-call(f32[128,128]{1,0:T(8,128)S(1)} %fusion.6), custom_call_target="Cholesky" | custom-call | tf_op jit(solution)/shard_map/jit(cholesky)/cholesky | solution.py:25
  868.8 9.8 custom-call.9
  878.8 1.1 fusion.19
  880.0 0.8 copy.19
  881.5 252.7 %all-reduce.17.cloned.1.call-done = f32[128,512]{1,0:T(8,128)} async-done(((f32[128,512]{1,0:T(8,128)}), f32[128,512]{1,0:T(8,128)}) %all-reduce.17.cloned.1.call-update) | async-done | bytes 262160 | tf_op jit(solution)/shard_map/psum | solution.py:29
  1134.1 1.7 copy.31
  (31 shorter events, 4.9 us)
Async XLA Ops:
  7.2 1.3 copy-start
  7.2 3.4 copy-start.1
  7.2 183.5 %all-reduce.7.cloned.1.call-start = ((), (), s32[]{:S(2)}) async-start(), calls=%async_computation.1 | async-start | bytes 131072 | tf_op jit(solution)/shard_map/psum | solution.py:13
  94.1 190.4 %all-reduce.9.cloned.1.call-start = ((), (), s32[]{:S(2)}) async-start(), calls=%async_computation.2 | async-start | bytes 131072 | tf_op jit(solution)/shard_map/psum | solution.py:13
  190.7 376.3 %all-reduce.11.cloned.1.call-start = ((), (), s32[]{:S(2)}) async-start(), calls=%async_computation.3 | async-start | bytes 524288 | tf_op jit(solution)/shard_map/psum | solution.py:29
  312.8 344.5 %reduce-scatter.2.cloned.1.call-start = ((), (), s32[]{:S(2)}) async-start(), calls=%async_computation.4 | async-start | bytes 5570560 | tf_op jit(solution)/shard_map/reduce_scatter | solution.py:56
  573.8 84.7 %copy-start.2 = (f32[512,128]{1,0:T(8,128)S(1)}, f32[512,128]{1,0:T(8,128)}, u32[]{:S(2)}) copy-start(f32[512,128]{1,0:T(8,128)} %param.7) | copy-start | bytes 786436
  573.8 186.5 %all-reduce.13.cloned.1.call-start = ((), (), s32[]{:S(2)}) async-start(), calls=%async_computation.5 | async-start | bytes 131072 | tf_op jit(solution)/shard_map/psum | solution.py:13
  660.0 193.9 %all-reduce.15.cloned.1.call-start = ((), (), s32[]{:S(2)}) async-start(), calls=%async_computation.6 | async-start | bytes 131072 | tf_op jit(solution)/shard_map/psum | solution.py:13
  760.3 373.8 %all-reduce.17.cloned.1.call-start = ((), (), s32[]{:S(2)}) async-start(), calls=%async_computation.7 | async-start | bytes 524288 | tf_op jit(solution)/shard_map/psum | solution.py:29
Sparse Core Ops, SparseCore 0:
  94.2 96.4 all-reduce.6
  193.8 90.5 all-reduce.8
  312.9 254.0 all-reduce.10
  573.9 83.3 reduce-scatter.1
  660.1 100.1 all-reduce.12
  763.3 90.5 all-reduce.14
  880.1 254.0 all-reduce.16
